TPU v7x, 32 devices: a whole 2x2x4 slice. The times are simulated.
32 devices in a mesh: view: 8 (over z, x), head: 4 (over y, core).
Axes of the slice: x: 2, y: 2, z: 4, core: 2. Of those that a mesh axis runs over, the one named last changes fastest.
Arguments:
- features: bfloat16 [16384, 1024], P(('view', 'head')), may hold values from -6 to 6
- attend_weight: bfloat16 [2, 3, 1024, 1024], P(None, None, 'view', 'head'), may hold values from -0.1875 to 0.1875
- output_weight: bfloat16 [2, 1024, 1024], P(None, 'view'), may hold values from -0.1875 to 0.1875
- fast_init: bfloat16 [2, 16, 3, 64, 512], P(None, 'head', None, None, 'view'), may hold values from -0.75 to 0.75
- update_mask: int32 [8, 2048], P('view'), may hold values 0 or 1
Outputs:
- refined: bfloat16 [16384, 1024], P(('view', 'head'))
All inputs are finite; a program needn't handle non-finite values. No bound on the sum of `update_mask` on one device may be relied on, other than what follows from the above.
Results may differ from a plain program's by a relative error of at most 0.035.
Values may be sent and summed in bfloat16 or wider, within the bound.
No kernel may reach another device: no remote copies, remote signals or barrier semaphores. Data moves between devices by JAX's collectives and lax.ppermute only.
A program may use at most 64 MiB of HBM per device.

v0:
```python
import jax
import jax.numpy as jnp
from jax import lax
from jax.sharding import PartitionSpec as P

BLOCKS = 2
NS_STEPS = 5
newton_coeffs = (3.4445, -4.775, 2.0315)
learn_rate = 1.0
score_scale = 0.25


def normalize(values, epsilon):
    return values * lax.rsqrt(jnp.mean(values * values, axis=-1, keepdims=True) + epsilon)


def newton_step(current, gram_matrix):
    squared = jnp.einsum(
        "...de,...ef->...df", gram_matrix, gram_matrix, precision=lax.Precision.HIGHEST
    )
    polynomial = newton_coeffs[1] * gram_matrix + newton_coeffs[2] * squared
    return newton_coeffs[0] * current + jnp.einsum(
        "...de,...ef->...df", polynomial, current, precision=lax.Precision.HIGHEST
    )


def self_gram(current):
    return jnp.einsum("...df,...ef->...de", current, current, precision=lax.Precision.HIGHEST)


def fast_gradient(keys, values, mask, weights):
    first = jnp.einsum("thd,hdf->thf", keys, weights[:, 0], preferred_element_type=jnp.float32)
    third = jnp.einsum("thd,hdf->thf", keys, weights[:, 1], preferred_element_type=jnp.float32)
    sigma = jax.nn.sigmoid(first)
    hidden = (first * sigma * third).astype(jnp.bfloat16)
    target = (-(mask[:, None, None].astype(jnp.float32) * values.astype(jnp.float32))).astype(
        jnp.bfloat16
    )
    back = jnp.einsum("thd,hdf->thf", target, weights[:, 2], preferred_element_type=jnp.float32)
    d_third = (back * first * sigma).astype(jnp.bfloat16)
    d_first = (back * third * sigma * (1.0 + first * (1.0 - sigma))).astype(jnp.bfloat16)
    grad_first = jnp.einsum("thd,thf->hdf", keys, d_first, preferred_element_type=jnp.float32)
    grad_third = jnp.einsum("thd,thf->hdf", keys, d_third, preferred_element_type=jnp.float32)
    grad_last = jnp.einsum("thd,thf->hdf", target, hidden, preferred_element_type=jnp.float32)
    return jnp.stack([grad_first, grad_third, grad_last], axis=1)


def fast_apply(queries, weights):
    first = jnp.einsum("thd,hdf->thf", queries, weights[:, 0], preferred_element_type=jnp.float32)
    third = jnp.einsum("thd,hdf->thf", queries, weights[:, 1], preferred_element_type=jnp.float32)
    hidden = (first * jax.nn.sigmoid(first) * third).astype(jnp.bfloat16)
    output = jnp.einsum("thf,hdf->thd", hidden, weights[:, 2], preferred_element_type=jnp.float32)
    return normalize(output, 1e-05)


def shards(features, attend_weight, output_weight, fast_init, update_mask):
    stream = features
    view_dev, view_len = update_mask.shape
    heads_here = fast_init.shape[1]
    head_dim = fast_init.shape[3]
    rows_all = view_dev * view_len
    block = min(512, view_len)
    count = rows_all // block
    mask_blocks = update_mask.reshape(count, block)
    for layer in range(BLOCKS):
        normed = normalize(stream.astype(jnp.float32), 1e-05).astype(jnp.bfloat16)
        whole = lax.all_gather(normed, "head", axis=0, tiled=True)
        packed = jnp.einsum(
            "td,jdc->tjc",
            whole,
            lax.all_gather(attend_weight[layer], "view", axis=1, tiled=True),
            preferred_element_type=jnp.float32,
        ).astype(jnp.bfloat16)
        packed = packed.reshape(rows_all, 3, heads_here, head_dim)
        queries = normalize(packed[:, 0].astype(jnp.float32), 1e-05).astype(jnp.bfloat16)
        keys = normalize(packed[:, 1].astype(jnp.float32), 1e-05).astype(jnp.bfloat16)
        values = packed[:, 2]
        key_views = keys.reshape(view_dev, view_len, heads_here, head_dim)
        value_views = values.reshape(view_dev, view_len, heads_here, head_dim)
        query_blocks = jnp.moveaxis(
            queries.reshape(view_dev, view_len // block, block, heads_here, head_dim), 1, 0
        )

        def attend_block(query_block):
            scores = (
                jnp.einsum(
                    "vqhd,vkhd->vhqk", query_block, key_views, preferred_element_type=jnp.float32
                )
                * score_scale
            )
            expo = jnp.exp(scores)
            probs = (expo / jnp.sum(expo, axis=-1, keepdims=True)).astype(jnp.bfloat16)
            return jnp.einsum(
                "vhqk,vkhd->vqhd", probs, value_views, preferred_element_type=jnp.float32
            )

        attended = jnp.moveaxis(lax.map(attend_block, query_blocks), 0, 1).reshape(
            rows_all, heads_here, head_dim
        )
        local_fast = fast_init[layer]
        full_fast = lax.all_gather(local_fast, "view", axis=3, tiled=True)

        def accumulate(total, inputs):
            return (total + fast_gradient(inputs[0], inputs[1], inputs[2], full_fast), None)

        key_blocks = keys.reshape(count, block, heads_here, head_dim)
        value_blocks = values.reshape(count, block, heads_here, head_dim)
        gradients, _ = lax.scan(
            accumulate,
            jnp.zeros(full_fast.shape, jnp.float32),
            (key_blocks, value_blocks, mask_blocks),
        )
        summed = lax.psum(gradients.astype(jnp.bfloat16), "view").astype(jnp.float32)
        squares = jnp.sum(summed * summed, axis=(2, 3), keepdims=True)
        current = summed * lax.rsqrt(squares + 1e-06)
        for _ in range(NS_STEPS):
            current = newton_step(current, self_gram(current))
        updated = (full_fast.astype(jnp.float32) - learn_rate * current).astype(jnp.bfloat16)

        def apply_block(query_block):
            return fast_apply(query_block, updated)

        applied = lax.map(apply_block, queries.reshape(count, block, heads_here, head_dim)).reshape(
            rows_all, heads_here, head_dim
        )
        mixed = (attended + applied).astype(jnp.bfloat16).reshape(rows_all, heads_here * head_dim)
        regrouped = lax.all_to_all(mixed, "head", split_axis=0, concat_axis=1, tiled=True)
        projected = jnp.dot(
            regrouped,
            lax.all_gather(output_weight[layer], "view", axis=0, tiled=True),
            preferred_element_type=jnp.float32,
        )
        stream = (stream.astype(jnp.float32) + projected).astype(jnp.bfloat16)
    return stream


def solution(mesh):
    return jax.shard_map(
        shards,
        mesh=mesh,
        in_specs=(
            P(("view", "head"), None),
            P(None, None, "view", "head"),
            P(None, "view", None),
            P(None, "head", None, None, "view"),
            P("view", None),
        ),
        out_specs=P(("view", "head"), None),
        check_vma=False,
    )
```

profile of v0, /device:TPU:0, one launch (start us, length us, event | category | flops | bytes accessed | tf_op | source)
XLA Modules:
  0.0 636.8 jit_solution(1773703120889669409)
XLA Ops:
  11.7 44.0 %all-gather.1 = bf16[1,4,3,64,512]{3,1,2,0,4:T(4,128)(2,1)} all-gather(bf16[1,4,3,64,64]{3,1,2,0,4:T(4,128)(2,1)S(1)} %copy.61), channel_id=3, replica_groups=mesh['view'=8,'head'=4] {'view'}, dimensions={4}, use_global_device_ids=true | all-gather | bytes 884736 | tf_op jit(solution)/shard_map/all_gather | solution.py:101
  59.5 6.3 all-gather.17.cloned.1.call-done
  65.8 35.9 %all-gather.13.cloned.1.call-done = bf16[2048,1024]{1,0:T(8,128)(2,1)} async-done(((bf16[512,1024]{1,0:T(8,128)(2,1)}), bf16[2048,1024]{1,0:T(8,128)(2,1)}) %all-gather.13.cloned.1.call-update) | async-done | bytes 4194320 | tf_op jit(solution)/shard_map/all_gather | solution.py:67
  101.7 6.1 fusion.188
  122.1 60.1 %while.66 = (s32[]{:T(128)}, f32[4,3,64,512]{3,2,0,1:T(8,128)S(1)}, bf16[4,512,4,64]{1,3,2,0:T(8,128)(2,1)}, s32[4,512]{1,0:T(4,128)S(1)}, bf16[4,512,4,64]{1,3,...) while((s32[]{:T(128)}, f32[4,3,64,512]{3,2,0,1:T(8,128)S(1)}, ...), condition=%wide.region_7.8_spmd.clone, body=%wide.region_6.7_spmd.clone.sunk | while | flops 830996992 | bytes 50605152 | solution.py:108
  199.0 31.0 %while.62 = (s32[]{:T(128)}, f32[4,1,512,4,64]{2,4,3,1,0:T(8,128)S(1)}, bf16[4,1,512,4,64]{2,4,3,1,0:T(8,128)(2,1)}, bf16[1,2048,4,64]{1,3,2,0:T(8,128)(2,1)S(1)}, bf16[1,2048,4,64]{1,3,2,0:T(8,128)(2,1)}, /*index=5*/s32[]{:T(128)}) while((s32[]{:T(128)}, f32[4,1,512,4,64]{2,4,3,1,0:T(8,128)S(1)}, bf16[4,1,512,4,64]{2,4,3,1,0:T(8,128)(2,1)}, ...), condition=%wide.region_5.6_spmd, body=%wide.region_3.5_spmd.sunk | while | flops 1094711296 | bytes 40649316 | solution.py:97
  230.0 28.5 %all-reduce.3.cloned.1.call-done = bf16[4,3,64,512]{3,2,1,0:T(8,128)(2,1)} async-done(((bf16[4,3,64,512]{3,2,1,0:T(8,128)(2,1)}), bf16[4,3,64,512]{3,2,1,0:T(8,128)(2,1)}) %all-reduce.3.cloned.1.call-update) | async-done | bytes 786448 | tf_op jit(solution)/shard_map/psum | solution.py:113
  283.2 35.3 %while.63 = (s32[]{:T(128)}, f32[4,512,4,64]{1,3,2,0:T(8,128)}, bf16[4,512,4,64]{1,3,2,0:T(8,128)(2,1)}, bf16[4,3,64,512]{3,2,0,1:T(8,128)(2,1)}, s32[]{:T(128)}) while((s32[]{:T(128)}, f32[4,512,4,64]{1,3,2,0:T(8,128)}, bf16[4,512,4,64]{1,3,2,0:T(8,128)(2,1)}, bf16[4,3,64,512]{3,2,0,1:T(8,128)(2,1)}, s32[]{:T(128)}) %tuple.131), condition=%wide.region_12.13_spmd, body=%wide.region_10.12_spmd.sunk | while | flops 409339904 | bytes 11306557 | solution.py:123
  287.0 4.1 multiply_reduce_fusion.8
  295.8 4.2 multiply_reduce_fusion.8
  313.4 4.2 multiply_reduce_fusion.8
  325.1 14.3 %all-to-all-done = bf16[4,512,256]{1,2,0:T(8,128)(2,1)S(1)} async-done(((bf16[4,512,256]{1,2,0:T(8,128)(2,1)}), bf16[4,512,256]{1,2,0:T(8,128)(2,1)S(1)}, u32[]{:S(2)}, u32[]{:S(2)}) %all-to-all-start) | async-done | bytes 1048608 | tf_op jit(solution)/shard_map/all_to_all | solution.py:127
  344.9 38.5 %all-gather.4 = bf16[1,4,3,64,512]{3,1,2,0,4:T(4,128)(2,1)} all-gather(bf16[1,4,3,64,64]{3,1,2,0,4:T(4,128)(2,1)S(1)} %copy.63), channel_id=6, replica_groups=mesh['view'=8,'head'=4] {'view'}, dimensions={4}, use_global_device_ids=true | all-gather | bytes 884736 | tf_op jit(solution)/shard_map/all_gather | solution.py:101
  386.2 5.2 all-gather.15.cloned.1.call-done
  391.5 6.1 fusion.191
  411.8 62.9 %while.67 = (s32[]{:T(128)}, f32[4,3,64,512]{3,2,0,1:T(8,128)S(1)}, bf16[4,512,4,64]{1,3,2,0:T(8,128)(2,1)}, s32[4,512]{1,0:T(4,128)}, bf16[4,512,4,64]{1,3,2,0:...) while((s32[]{:T(128)}, f32[4,3,64,512]{3,2,0,1:T(8,128)S(1)}, ...), condition=%wide.region_20.21_spmd.clone, body=%wide.region_19.20_spmd.clone.sunk | while | flops 830996992 | bytes 50605152 | solution.py:108
  491.3 34.0 %while.64 = (s32[]{:T(128)}, f32[4,1,512,4,64]{2,4,3,1,0:T(8,128)}, bf16[4,1,512,4,64]{2,4,3,1,0:T(8,128)(2,1)}, bf16[1,2048,4,64]{1,3,2,0:T(8,128)(2,1)S(1)}, bf16[1,2048,4,64]{1,3,2,0:T(8,128)(2,1)}, /*index=5*/s32[]{:T(128)}) while((s32[]{:T(128)}, f32[4,1,512,4,64]{2,4,3,1,0:T(8,128)}, bf16[4,1,512,4,64]{2,4,3,1,0:T(8,128)(2,1)}, ...), condition=%wide.region_18.19_spmd, body=%wide.region_16.18_spmd.sunk | while | flops 1094711296 | bytes 40649824 | solution.py:97
  495.4 4.3 fusion.377
  503.8 4.3 fusion.377
  512.2 4.3 fusion.377
  520.5 4.3 fusion.377
  526.9 24.3 %all-reduce.5.cloned.1.call-done = bf16[4,3,64,512]{3,2,1,0:T(8,128)(2,1)} async-done(((bf16[4,3,64,512]{3,2,1,0:T(8,128)(2,1)}), bf16[4,3,64,512]{3,2,1,0:T(8,128)(2,1)}) %all-reduce.5.cloned.1.call-update) | async-done | bytes 786448 | tf_op jit(solution)/shard_map/psum | solution.py:113
  573.2 31.6 %while.65 = (s32[]{:T(128)}, f32[4,512,4,64]{1,3,2,0:T(8,128)S(1)}, bf16[4,512,4,64]{1,3,2,0:T(8,128)(2,1)}, bf16[4,3,64,512]{3,2,0,1:T(8,128)(2,1)S(1)}, s32[]{:T(128)}) while((s32[]{:T(128)}, f32[4,512,4,64]{1,3,2,0:T(8,128)S(1)}, bf16[4,512,4,64]{1,3,2,0:T(8,128)(2,1)}, bf16[4,3,64,512]{3,2,0,1:T(8,128)(2,1)S(1)}, s32[]{:T(128)}) %tuple.140), condition=%wide.region_25.26_spmd, body=%wide.region_23.25_spmd.sunk | while | flops 409339904 | bytes 11306049 | solution.py:123
  611.6 14.4 %all-to-all-done.1 = bf16[4,512,256]{1,2,0:T(8,128)(2,1)S(1)} async-done(((bf16[4,512,256]{1,2,0:T(8,128)(2,1)}), bf16[4,512,256]{1,2,0:T(8,128)(2,1)S(1)}, u32[]{:S(2)}, u32[]{:S(2)}) %all-to-all-start.1) | async-done | bytes 1048608 | tf_op jit(solution)/shard_map/all_to_all | solution.py:127
  (284 shorter events, 367.8 us)
Async XLA Ops:
  6.5 59.3 %all-gather.17.cloned.1.call-start = ((), (), s32[]{:S(2)}) async-start(), calls=%async_computation.6 | async-start | bytes 1769472 | tf_op jit(solution)/shard_map/all_gather | solution.py:71
  9.2 92.5 %all-gather.13.cloned.1.call-start = ((), (), s32[]{:S(2)}) async-start(), calls=%async_computation.2 | async-start | bytes 5242880 | tf_op jit(solution)/shard_map/all_gather | solution.py:67
  10.8 247.8 %all-reduce.3.cloned.1.call-start = ((), (), s32[]{:S(2)}) async-start(), calls=%async_computation.3 | async-start | bytes 1572864 | tf_op jit(solution)/shard_map/psum | solution.py:113
  11.7 47.1 %copy-start.22 = (s32[1,2048]{1,0:T(1,128)S(1)}, s32[1,2048]{1,0:T(1,128)}, u32[]{:S(2)}) copy-start(s32[1,2048]{1,0:T(1,128)} %param.21) | copy-start | bytes 24580
  183.3 5.4 copy-start
  183.3 141.8 %all-gather.19.cloned.1.call-start = ((), (), s32[]{:S(2)}) async-start(), calls=%async_computation.7 | async-start | bytes 2359296 | tf_op jit(solution)/shard_map/all_gather | solution.py:130
  184.3 202.0 %all-gather.21.cloned.1.call-start = ((), (), s32[]{:S(2)}) async-start(), calls=%async_computation.8 | async-start | bytes 1769472 | tf_op jit(solution)/shard_map/all_gather | solution.py:71
  199.0 4.1 copy-start.13
  206.8 4.1 copy-start.13
  214.5 4.1 copy-start.13
  222.3 4.1 copy-start.13
  258.6 5.3 copy-start.11
  321.4 18.1 %copy-start.8 = (bf16[512,1024]{1,0:T(8,128)(2,1)S(1)}, bf16[512,1024]{1,0:T(8,128)(2,1)}, u32[]{:S(2)}) copy-start(bf16[512,1024]{1,0:T(8,128)(2,1)} %param.17) | copy-start | bytes 3145732
  321.4 18.1 %all-to-all-start = ((bf16[4,512,256]{1,2,0:T(8,128)(2,1)}), bf16[4,512,256]{1,2,0:T(8,128)(2,1)S(1)}, u32[]{:S(2)}, u32[]{:S(2)}) async-start(bf16[4,512,256]{1,2,0:T(8,128)(2,1)} %fusion.206), calls=%async_computation | async-start | bytes 2097152 | tf_op jit(solution)/shard_map/all_to_all | solution.py:127
  325.1 66.4 %all-gather.15.cloned.1.call-start = ((), (), s32[]{:S(2)}) async-start(), calls=%async_computation.4 | async-start | bytes 5242880 | tf_op jit(solution)/shard_map/all_gather | solution.py:67
  344.7 206.5 %all-reduce.5.cloned.1.call-start = ((), (), s32[]{:S(2)}) async-start(), calls=%async_computation.5 | async-start | bytes 1572864 | tf_op jit(solution)/shard_map/psum | solution.py:113
  475.8 135.8 %all-gather.23.cloned.1.call-start = ((), (), s32[]{:S(2)}) async-start(), calls=%async_computation.9 | async-start | bytes 2359296 | tf_op jit(solution)/shard_map/all_gather | solution.py:130
  476.5 5.1 copy-start.1
  491.3 34.0 %copy-start.4 = (f32[4,512,4,64]{1,0,3,2:T(4,128)S(1)}, f32[4,512,4,64]{1,0,3,2:T(4,128)}, u32[]{:S(2)}) copy-start(f32[4,512,4,64]{1,0,3,2:T(4,128)} %reshape.326) | copy-start | bytes 6291460
  491.3 4.1 copy-start.14
  508.1 4.0 copy-start.14
  551.1 5.2 copy-start.12
  607.9 18.1 %copy-start.16 = (bf16[512,1024]{1,0:T(8,128)(2,1)S(1)}, bf16[512,1024]{1,0:T(8,128)(2,1)}, u32[]{:S(2)}) copy-start(bf16[512,1024]{1,0:T(8,128)(2,1)} %copy-done.15) | copy-start | bytes 3145732
  607.9 18.1 %all-to-all-start.1 = ((bf16[4,512,256]{1,2,0:T(8,128)(2,1)}), bf16[4,512,256]{1,2,0:T(8,128)(2,1)S(1)}, u32[]{:S(2)}, u32[]{:S(2)}) async-start(bf16[4,512,256]{1,2,0:T(8,128)(2,1)} %fusion.202), calls=%async_computation.1 | async-start | bytes 2097152 | tf_op jit(solution)/shard_map/all_to_all | solution.py:127
  (15 other events, 35.6 us)
Sparse Core Ops, SparseCore 0:
  9.4 56.3 all-gather.16
  67.4 34.3 all-gather.12
  183.4 75.1 all-reduce.2
  260.6 48.2 all-gather.18
  310.8 45.6 all-gather.20
  357.8 33.5 all-gather.14
  475.9 75.2 all-reduce.4
  553.2 48.2 all-gather.22
where the time goes:
time: 649 us; the launch traced here: 637 us
  matrix products  294 us (45%)
  waiting for transfers between devices  130 us (20%)
  blocking collectives  82.5 us (13%)
  local copies, waits for them, and re-layouts  56.3 us (9%)
  other arithmetic  50.9 us (8%)
  between operations  14.3 us (2%)
  starting transfers between devices  7.77 us (1%)
    all_gather x2, blocking collectives, shards(): full_fast = lax.all_gather(local_fast, 'view', axis=3, tiled=True)  82.5 us
    psum x2, waiting for transfers between devices, shards(): lax.psum(gradients.astype(jnp.bfloat16), 'view').astype(jnp.float32)  52.8 us
    all_gather x2, waiting for transfers between devices, shards(): whole = lax.all_gather(normed, 'head', axis=0, tiled=True)  41.2 us
    dot_general x8, matrix products, fast_apply(): jnp.einsum('thf,hdf->thd', hidden, weights[:, 2], preferred_element_type=...  33 us
    dot_general x8, matrix products, attend_block(): jnp.einsum('vqhd,vkhd->vhqk', query_block, key_views, preferred_element_t...  32.4 us
    dot_general x8, matrix products, attend_block(): jnp.einsum('vhqk,vkhd->vqhd', probs, value_views, preferred_element_type=...  31.9 us
    dot_general x8, matrix products, fast_apply(): jnp.einsum('thd,hdf->thf', queries, weights[:, 0], preferred_element_type...  29.9 us
    all_to_all x2, waiting for transfers between devices, shards(): lax.all_to_all(mixed, 'head', split_axis=0, concat_axis=1, tiled=True)  28.7 us
  transfers between devices with their start and end apart: 10, of which 7 were waited for; matrix products, arithmetic and copies ran while one was open for 36% of the time, Pallas kernels for 0%

commit v1 on v0

--- a/solution.py
+++ b/solution.py
@@ -64,7 +64,13 @@
     mask_blocks = update_mask.reshape(count, block)
     for layer in range(BLOCKS):
         normed = normalize(stream.astype(jnp.float32), 1e-05).astype(jnp.bfloat16)
-        whole = lax.all_gather(normed, "head", axis=0, tiled=True)
+        size = lax.axis_size("head")
+        held, shards_2 = (normed, [normed])
+        for _ in range(size - 1):
+            held = lax.ppermute(held, "head", [(i, (i + 1) % size) for i in range(size)])
+            shards_2.insert(0, held)
+        line = jnp.concatenate(shards_2, axis=0)
+        whole = jnp.roll(line, (lax.axis_index("head") + 1) * normed.shape[0], axis=0)
         packed = jnp.einsum(
             "td,jdc->tjc",
             whole,

time: 649 us -> 665 us (1.025)
  matrix products: 294 us -> 309 us
    ppermute x0 -> x6, waiting for transfers between devices: none -> 54.8 us  [shards(): lax.ppermute(held, 'head', [(i, (i + 1) % size) for i in range(size)])]
    all_gather x2 -> x0, waiting for transfers between devices: 41.2 us -> none  [shards(): whole = lax.all_gather(normed, 'head', axis=0, tiled=True)]
    dot_general x2, matrix products: 12.2 us -> 25.7 us  [shards(): jnp.einsum('td,jdc->tjc', whole, lax.all_gather(attend_weight[layer], 'vi...]
  transfers between devices with their start and end apart: 10 -> 14, of which waited for: 7 -> 8; matrix products, arithmetic and copies ran while one was open for 36% -> 34% of each run, Pallas kernels for 0% -> 0%
where the time goes in v1:
time: 665 us; the launch traced here: 654 us
  matrix products  309 us (46%)
  waiting for transfers between devices  131 us (20%)
  blocking collectives  84.6 us (13%)
  local copies, waits for them, and re-layouts  54.2 us (8%)
  other arithmetic  49.9 us (8%)
  between operations  14.4 us (2%)
  starting transfers between devices  8.27 us (1%)
    all_gather x2, blocking collectives, shards(): full_fast = lax.all_gather(local_fast, 'view', axis=3, tiled=True)  84.6 us
    ppermute x6, waiting for transfers between devices, shards(): lax.ppermute(held, 'head', [(i, (i + 1) % size) for i in range(size)])  54.8 us
    psum x2, waiting for transfers between devices, shards(): lax.psum(gradients.astype(jnp.bfloat16), 'view').astype(jnp.float32)  47.3 us
    dot_general x8, matrix products, attend_block(): jnp.einsum('vhqk,vkhd->vqhd', probs, value_views, preferred_element_type=...  34.6 us
    dot_general x8, matrix products, fast_apply(): jnp.einsum('thf,hdf->thd', hidden, weights[:, 2], preferred_element_type=...  32.7 us
    dot_general x8, matrix products, attend_block(): jnp.einsum('vqhd,vkhd->vhqk', query_block, key_views, preferred_element_t...  32.4 us
    dot_general x8, matrix products, fast_apply(): jnp.einsum('thd,hdf->thf', queries, weights[:, 0], preferred_element_type...  29.2 us
    all_to_all x2, waiting for transfers between devices, shards(): lax.all_to_all(mixed, 'head', split_axis=0, concat_axis=1, tiled=True)  28.7 us
  transfers between devices with their start and end apart: 14, of which 8 were waited for; matrix products, arithmetic and copies ran while one was open for 34% of the time, Pallas kernels for 0%

profile of v1, /device:TPU:0, one launch (start us, length us, event | category | flops | bytes accessed | tf_op | source)
XLA Modules:
  0.0 653.7 jit_solution(12199085395694789830)
XLA Ops:
  11.7 12.8 %collective-permute-done = bf16[512,1024]{1,0:T(8,128)(2,1)S(1)} collective-permute-done((bf16[512,1024]{1,0:T(8,128)(2,1)S(1)}, bf16[512,1024]{1,0:T(8,128)(2,1)S(1)}, u32[]{:S(2)}, u32[]{:S(2)}) %collective-permute-start) | collective-permute-done | bytes 1048608 | tf_op jit(solution)/shard_map/ppermute | solution.py:70
  24.6 14.3 %collective-permute-done.1 = bf16[512,1024]{1,0:T(8,128)(2,1)} collective-permute-done((bf16[512,1024]{1,0:T(8,128)(2,1)S(1)}, bf16[512,1024]{1,0:T(8,128)(2,1)}, u32[]{:S(2)}, u32[]{:S(2)}) %collective-permute-start.1) | collective-permute-done | bytes 1048608 | tf_op jit(solution)/shard_map/ppermute | solution.py:70
  39.8 43.3 %all-gather.1 = bf16[1,4,3,64,512]{3,1,2,0,4:T(4,128)(2,1)} all-gather(bf16[1,4,3,64,64]{3,1,2,0,4:T(4,128)(2,1)S(1)} %copy.61), channel_id=3, replica_groups=mesh['view'=8,'head'=4] {'view'}, dimensions={4}, use_global_device_ids=true | all-gather | bytes 884736 | tf_op jit(solution)/shard_map/all_gather | solution.py:107
  87.0 12.9 %fusion.206 = bf16[2048,3,256]{0,2,1:T(8,128)(2,1)S(1)} fusion(s32[]{:T(128)S(6)} %select_n.13, bf16[512,1024]{1,0:T(8,128)(2,1)} %collective-permute-done.2, bf16[512,1024]{1,0:T(8,128)(2,1)} %collective-permute-done.1, bf16[512,1024]{1,0:T(8,128)(2,1)} %copy-done.22, bf16[512,1024]{1,0:T(8,128)(2,1)S(1)} %fusion.213, ...), kind=kOutput, calls=%fused_computation.218 | convolution fusion | flops 3256352768 | bytes 8912900 | tf_op jit(solution)/shard_map/td,jdc->tjc/dot_general | solution.py:74
  114.2 60.3 %while.66 = (s32[]{:T(128)}, f32[4,3,64,512]{3,2,0,1:T(8,128)S(1)}, bf16[4,512,4,64]{1,3,2,0:T(8,128)(2,1)}, s32[4,512]{1,0:T(4,128)S(1)}, bf16[4,512,4,64]{1,3,...) while((s32[]{:T(128)}, f32[4,3,64,512]{3,2,0,1:T(8,128)S(1)}, ...), condition=%wide.region_7.9_spmd.clone, body=%wide.region_6.8_spmd.clone.sunk | while | flops 830996992 | bytes 50605152 | solution.py:114
  191.3 33.7 %while.62 = (s32[]{:T(128)}, f32[4,1,512,4,64]{2,4,3,1,0:T(8,128)}, bf16[4,1,512,4,64]{2,4,3,1,0:T(8,128)(2,1)}, bf16[1,2048,4,64]{1,3,2,0:T(8,128)(2,1)S(1)}, bf16[1,2048,4,64]{1,3,2,0:T(8,128)(2,1)}, /*index=5*/s32[]{:T(128)}) while((s32[]{:T(128)}, f32[4,1,512,4,64]{2,4,3,1,0:T(8,128)}, bf16[4,1,512,4,64]{2,4,3,1,0:T(8,128)(2,1)}, ...), condition=%wide.region_5.7_spmd, body=%wide.region_3.6_spmd.sunk | while | flops 1094711296 | bytes 40649824 | solution.py:103
  203.8 4.3 fusion.391
  212.2 4.3 fusion.391
  220.6 4.3 fusion.391
  226.7 24.6 %all-reduce.3.cloned.1.call-done = bf16[4,3,64,512]{3,2,1,0:T(8,128)(2,1)} async-done(((bf16[4,3,64,512]{3,2,1,0:T(8,128)(2,1)}), bf16[4,3,64,512]{3,2,1,0:T(8,128)(2,1)}) %all-reduce.3.cloned.1.call-update) | async-done | bytes 786448 | tf_op jit(solution)/shard_map/psum | solution.py:119
  273.6 31.4 %while.63 = (s32[]{:T(128)}, f32[4,512,4,64]{1,3,2,0:T(8,128)S(1)}, bf16[4,512,4,64]{1,3,2,0:T(8,128)(2,1)}, bf16[4,3,64,512]{3,2,0,1:T(8,128)(2,1)S(1)}, s32[]{:T(128)}) while((s32[]{:T(128)}, f32[4,512,4,64]{1,3,2,0:T(8,128)S(1)}, bf16[4,512,4,64]{1,3,2,0:T(8,128)(2,1)}, bf16[4,3,64,512]{3,2,0,1:T(8,128)(2,1)S(1)}, s32[]{:T(128)}) %tuple.132), condition=%wide.region_12.14_spmd, body=%wide.region_10.13_spmd.sunk | while | flops 409339904 | bytes 11306049 | solution.py:129
  311.7 14.3 %all-to-all-done = bf16[4,512,256]{1,2,0:T(8,128)(2,1)S(1)} async-done(((bf16[4,512,256]{1,2,0:T(8,128)(2,1)}), bf16[4,512,256]{1,2,0:T(8,128)(2,1)S(1)}, u32[]{:S(2)}, u32[]{:S(2)}) %all-to-all-start) | async-done | bytes 1048608 | tf_op jit(solution)/shard_map/all_to_all | solution.py:133
  331.2 13.3 %collective-permute-done.3 = bf16[512,1024]{1,0:T(8,128)(2,1)S(1)} collective-permute-done((bf16[512,1024]{1,0:T(8,128)(2,1)S(1)}, bf16[512,1024]{1,0:T(8,128)(2,1)S(1)}, u32[]{:S(2)}, u32[]{:S(2)}) %collective-permute-start.3) | collective-permute-done | bytes 1048608 | tf_op jit(solution)/shard_map/ppermute | solution.py:70
  344.5 14.3 %collective-permute-done.4 = bf16[512,1024]{1,0:T(8,128)(2,1)} collective-permute-done((bf16[512,1024]{1,0:T(8,128)(2,1)S(1)}, bf16[512,1024]{1,0:T(8,128)(2,1)}, u32[]{:S(2)}, u32[]{:S(2)}) %collective-permute-start.4) | collective-permute-done | bytes 1048608 | tf_op jit(solution)/shard_map/ppermute | solution.py:70
  359.2 41.4 %all-gather.4 = bf16[1,4,3,64,512]{3,1,2,0,4:T(4,128)(2,1)} all-gather(bf16[1,4,3,64,64]{3,1,2,0,4:T(4,128)(2,1)S(1)} %copy.63), channel_id=6, replica_groups=mesh['view'=8,'head'=4] {'view'}, dimensions={4}, use_global_device_ids=true | all-gather | bytes 884736 | tf_op jit(solution)/shard_map/all_gather | solution.py:107
  403.2 12.9 %fusion.209 = bf16[2048,3,256]{0,2,1:T(8,128)(2,1)S(1)} fusion(s32[]{:T(128)S(6)} %select_n.13, bf16[512,1024]{1,0:T(8,128)(2,1)} %collective-permute-done.5, bf16[512,1024]{1,0:T(8,128)(2,1)} %collective-permute-done.4, bf16[512,1024]{1,0:T(8,128)(2,1)} %copy-done.23, bf16[512,1024]{1,0:T(8,128)(2,1)S(1)} %fusion.216, ...), kind=kOutput, calls=%fused_computation.219 | convolution fusion | flops 3256352768 | bytes 8912900 | tf_op jit(solution)/shard_map/td,jdc->tjc/dot_general | solution.py:74
  430.3 63.1 %while.67 = (s32[]{:T(128)}, f32[4,3,64,512]{3,2,0,1:T(8,128)S(1)}, bf16[4,512,4,64]{1,3,2,0:T(8,128)(2,1)}, s32[4,512]{1,0:T(4,128)}, bf16[4,512,4,64]{1,3,2,0:...) while((s32[]{:T(128)}, f32[4,3,64,512]{3,2,0,1:T(8,128)S(1)}, ...), condition=%wide.region_20.22_spmd.clone, body=%wide.region_19.21_spmd.clone.sunk | while | flops 830996992 | bytes 50605152 | solution.py:114
  509.9 33.9 %while.64 = (s32[]{:T(128)}, f32[4,1,512,4,64]{2,4,3,1,0:T(8,128)}, bf16[4,1,512,4,64]{2,4,3,1,0:T(8,128)(2,1)}, bf16[1,2048,4,64]{1,3,2,0:T(8,128)(2,1)S(1)}, bf16[1,2048,4,64]{1,3,2,0:T(8,128)(2,1)}, /*index=5*/s32[]{:T(128)}) while((s32[]{:T(128)}, f32[4,1,512,4,64]{2,4,3,1,0:T(8,128)}, bf16[4,1,512,4,64]{2,4,3,1,0:T(8,128)(2,1)}, ...), condition=%wide.region_18.20_spmd, body=%wide.region_16.19_spmd.sunk | while | flops 1094711296 | bytes 40649824 | solution.py:103
  522.3 4.3 fusion.399
  530.7 4.3 fusion.399
  539.1 4.3 fusion.399
  545.5 22.8 %all-reduce.5.cloned.1.call-done = bf16[4,3,64,512]{3,2,1,0:T(8,128)(2,1)} async-done(((bf16[4,3,64,512]{3,2,1,0:T(8,128)(2,1)}), bf16[4,3,64,512]{3,2,1,0:T(8,128)(2,1)}) %all-reduce.5.cloned.1.call-update) | async-done | bytes 786448 | tf_op jit(solution)/shard_map/psum | solution.py:119
  590.3 31.3 %while.65 = (s32[]{:T(128)}, f32[4,512,4,64]{1,3,2,0:T(8,128)S(1)}, bf16[4,512,4,64]{1,3,2,0:T(8,128)(2,1)}, bf16[4,3,64,512]{3,2,0,1:T(8,128)(2,1)S(1)}, s32[]{:T(128)}) while((s32[]{:T(128)}, f32[4,512,4,64]{1,3,2,0:T(8,128)S(1)}, bf16[4,512,4,64]{1,3,2,0:T(8,128)(2,1)}, bf16[4,3,64,512]{3,2,0,1:T(8,128)(2,1)S(1)}, s32[]{:T(128)}) %tuple.141), condition=%wide.region_25.27_spmd, body=%wide.region_23.26_spmd.sunk | while | flops 409339904 | bytes 11306049 | solution.py:129
  628.4 14.4 %all-to-all-done.1 = bf16[4,512,256]{1,2,0:T(8,128)(2,1)S(1)} async-done(((bf16[4,512,256]{1,2,0:T(8,128)(2,1)}), bf16[4,512,256]{1,2,0:T(8,128)(2,1)S(1)}, u32[]{:S(2)}, u32[]{:S(2)}) %all-to-all-start.1) | async-done | bytes 1048608 | tf_op jit(solution)/shard_map/all_to_all | solution.py:133
  (292 shorter events, 370.5 us)
Async XLA Ops:
  6.5 32.4 %copy-start.19 = (bf16[2,4,3,64,64]{4,3,2,1,0:T(8,128)(2,1)S(1)}, bf16[2,4,3,64,64]{4,3,2,1,0:T(8,128)(2,1)}, u32[]{:S(2)}) copy-start(bf16[2,4,3,64,64]{4,3,2,1,0:T(8,128)(2,1)} %param.22) | copy-start | bytes 589828
  6.5 80.4 %all-gather.11.cloned.1.call-start = ((), (), s32[]{:S(2)}) async-start(), calls=%async_computation.4 | async-start | bytes 1769472 | tf_op jit(solution)/shard_map/all_gather | solution.py:77
  9.6 15.0 %collective-permute-start = (bf16[512,1024]{1,0:T(8,128)(2,1)S(1)}, bf16[512,1024]{1,0:T(8,128)(2,1)S(1)}, u32[]{:S(2)}, u32[]{:S(2)}) collective-permute-start(bf16[512,1024]{1,0:T(8,128)(2,1)S(1)} %fusion.213), channel_id=1, source_target_pairs={{0,1},{1,2},{2,3},{3,0},{4,5},{5,6},{6,7},{7,4},{8,9},{9,10},{10,1... | collective-permute-start | bytes 3145736 | tf_op jit(solution)/shard_map/ppermute | solution.py:70
  11.7 239.5 %all-reduce.3.cloned.1.call-start = ((), (), s32[]{:S(2)}) async-start(), calls=%async_computation.2 | async-start | bytes 1572864 | tf_op jit(solution)/shard_map/psum | solution.py:119
  24.6 14.3 %copy-start.22 = (bf16[512,1024]{1,0:T(8,128)(2,1)}, bf16[512,1024]{1,0:T(8,128)(2,1)S(1)}, u32[]{:S(2)}) copy-start(bf16[512,1024]{1,0:T(8,128)(2,1)S(1)} %collective-permute-done) | copy-start | bytes 3145732
  24.6 14.3 %collective-permute-start.1 = (bf16[512,1024]{1,0:T(8,128)(2,1)S(1)}, bf16[512,1024]{1,0:T(8,128)(2,1)}, u32[]{:S(2)}, u32[]{:S(2)}) collective-permute-start(bf16[512,1024]{1,0:T(8,128)(2,1)S(1)} %collective-permute-done), channel_id=1, source_target_pairs={{0,1},{1,2},{2,3},{3,0},{4,5},{5,6},{6,7},{7,4},{8,9},{9,10},{10,1... | collective-permute-start | bytes 3145736 | tf_op jit(solution)/shard_map/ppermute | solution.py:70
  38.9 48.1 %collective-permute-start.2 = (bf16[512,1024]{1,0:T(8,128)(2,1)}, bf16[512,1024]{1,0:T(8,128)(2,1)}, u32[]{:S(2)}, u32[]{:S(2)}) collective-permute-start(bf16[512,1024]{1,0:T(8,128)(2,1)} %collective-permute-done.1), channel_id=1, source_target_pairs={{0,1},{1,2},{2,3},{3,0},{4,5},{5,6},{6,7},{7,4},{8,9},{9,10},{10,1... | collective-permute-start | bytes 3145736 | tf_op jit(solution)/shard_map/ppermute | solution.py:70
  39.8 46.5 %copy-start.21 = (s32[1,2048]{1,0:T(1,128)S(1)}, s32[1,2048]{1,0:T(1,128)}, u32[]{:S(2)}) copy-start(s32[1,2048]{1,0:T(1,128)} %param.23) | copy-start | bytes 24580
  175.6 136.1 %all-gather.13.cloned.1.call-start = ((), (), s32[]{:S(2)}) async-start(), calls=%async_computation.5 | async-start | bytes 2359296 | tf_op jit(solution)/shard_map/all_gather | solution.py:136
  191.3 33.8 %copy-start.5 = (f32[4,512,4,64]{1,0,3,2:T(4,128)S(1)}, f32[4,512,4,64]{1,0,3,2:T(4,128)}, u32[]{:S(2)}) copy-start(f32[4,512,4,64]{1,0,3,2:T(4,128)} %reshape.322) | copy-start | bytes 6291460
  308.0 18.1 %copy-start.6 = (bf16[512,1024]{1,0:T(8,128)(2,1)S(1)}, bf16[512,1024]{1,0:T(8,128)(2,1)}, u32[]{:S(2)}) copy-start(bf16[512,1024]{1,0:T(8,128)(2,1)} %param.19) | copy-start | bytes 3145732
  308.0 18.1 %all-to-all-start = ((bf16[4,512,256]{1,2,0:T(8,128)(2,1)}), bf16[4,512,256]{1,2,0:T(8,128)(2,1)S(1)}, u32[]{:S(2)}, u32[]{:S(2)}) async-start(bf16[4,512,256]{1,2,0:T(8,128)(2,1)} %fusion.224), calls=%async_computation | async-start | bytes 2097152 | tf_op jit(solution)/shard_map/all_to_all | solution.py:133
  311.6 91.5 %all-gather.15.cloned.1.call-start = ((), (), s32[]{:S(2)}) async-start(), calls=%async_computation.6 | async-start | bytes 1769472 | tf_op jit(solution)/shard_map/all_gather | solution.py:77
  329.0 30.0 %copy-start.16 = (bf16[1,4,3,64,64]{4,3,2,1,0:T(8,128)(2,1)S(1)}, bf16[1,4,3,64,64]{4,3,2,1,0:T(8,128)(2,1)}, u32[]{:S(2)}) copy-start(bf16[1,4,3,64,64]{4,3,2,1,0:T(8,128)(2,1)} %get-tuple-element.358) | copy-start | bytes 294916
  330.2 14.3 %collective-permute-start.3 = (bf16[512,1024]{1,0:T(8,128)(2,1)S(1)}, bf16[512,1024]{1,0:T(8,128)(2,1)S(1)}, u32[]{:S(2)}, u32[]{:S(2)}) collective-permute-start(bf16[512,1024]{1,0:T(8,128)(2,1)S(1)} %fusion.216), channel_id=1, source_target_pairs={{0,1},{1,2},{2,3},{3,0},{4,5},{5,6},{6,7},{7,4},{8,9},{9,10},{10,1... | collective-permute-start | bytes 3145736 | tf_op jit(solution)/shard_map/ppermute | solution.py:70
  331.1 237.1 %all-reduce.5.cloned.1.call-start = ((), (), s32[]{:S(2)}) async-start(), calls=%async_computation.3 | async-start | bytes 1572864 | tf_op jit(solution)/shard_map/psum | solution.py:119
  344.5 14.3 %copy-start.23 = (bf16[512,1024]{1,0:T(8,128)(2,1)}, bf16[512,1024]{1,0:T(8,128)(2,1)S(1)}, u32[]{:S(2)}) copy-start(bf16[512,1024]{1,0:T(8,128)(2,1)S(1)} %collective-permute-done.3) | copy-start | bytes 3145732
  344.5 14.3 %collective-permute-start.4 = (bf16[512,1024]{1,0:T(8,128)(2,1)S(1)}, bf16[512,1024]{1,0:T(8,128)(2,1)}, u32[]{:S(2)}, u32[]{:S(2)}) collective-permute-start(bf16[512,1024]{1,0:T(8,128)(2,1)S(1)} %collective-permute-done.3), channel_id=1, source_target_pairs={{0,1},{1,2},{2,3},{3,0},{4,5},{5,6},{6,7},{7,4},{8,9},{9,10},{10,1... | collective-permute-start | bytes 3145736 | tf_op jit(solution)/shard_map/ppermute | solution.py:70
  358.8 44.3 %collective-permute-start.5 = (bf16[512,1024]{1,0:T(8,128)(2,1)}, bf16[512,1024]{1,0:T(8,128)(2,1)}, u32[]{:S(2)}, u32[]{:S(2)}) collective-permute-start(bf16[512,1024]{1,0:T(8,128)(2,1)} %collective-permute-done.4), channel_id=1, source_target_pairs={{0,1},{1,2},{2,3},{3,0},{4,5},{5,6},{6,7},{7,4},{8,9},{9,10},{10,1... | collective-permute-start | bytes 3145736 | tf_op jit(solution)/shard_map/ppermute | solution.py:70
  494.4 134.0 %all-gather.17.cloned.1.call-start = ((), (), s32[]{:S(2)}) async-start(), calls=%async_computation.7 | async-start | bytes 2359296 | tf_op jit(solution)/shard_map/all_gather | solution.py:136
  509.9 33.9 %copy-start.4 = (f32[4,512,4,64]{1,0,3,2:T(4,128)S(1)}, f32[4,512,4,64]{1,0,3,2:T(4,128)}, u32[]{:S(2)}) copy-start(f32[4,512,4,64]{1,0,3,2:T(4,128)} %reshape.326) | copy-start | bytes 6291460
  568.2 5.2 copy-start.10
  624.8 18.1 %copy-start.14 = (bf16[512,1024]{1,0:T(8,128)(2,1)S(1)}, bf16[512,1024]{1,0:T(8,128)(2,1)}, u32[]{:S(2)}) copy-start(bf16[512,1024]{1,0:T(8,128)(2,1)} %copy-done.13) | copy-start | bytes 3145732
  624.8 18.1 %all-to-all-start.1 = ((bf16[4,512,256]{1,2,0:T(8,128)(2,1)}), bf16[4,512,256]{1,2,0:T(8,128)(2,1)S(1)}, u32[]{:S(2)}, u32[]{:S(2)}) async-start(bf16[4,512,256]{1,2,0:T(8,128)(2,1)} %fusion.220), calls=%async_computation.1 | async-start | bytes 2097152 | tf_op jit(solution)/shard_map/all_to_all | solution.py:133
  (20 other events, 67.6 us)
Sparse Core Ops, SparseCore 0:
  11.8 59.8 all-gather.10
  175.7 75.5 all-reduce.2
  253.4 48.2 all-gather.12
  331.3 55.7 all-gather.14
  494.5 73.6 all-reduce.4
  570.2 48.2 all-gather.16
